TPU v7x, 256 devices: a whole 4x4x8 slice. The times are simulated.
256 devices in a mesh: dp: 16 (over y, x), cluster: 16 (over z, core).
Axes of the slice: x: 4, y: 4, z: 8, core: 2. Of those that a mesh axis runs over, the one named last changes fastest.
Arguments:
- points: bfloat16 [524288, 768], P(('dp', 'cluster')), may hold values from -12 to 12
- coarse_id: int32 [524288, 1], P(('dp', 'cluster')), may hold values from 0 to 255; in each aligned block of 2048 rows (0 to 2047, 2048 to 4095, ...) at most 24 rows name the same one
- owner_map: int32 [256], replicated, may hold values from 0 to 255, each once
- centroids: bfloat16 [256, 256, 768], P('cluster', 'dp'), may hold values from -1 to 1
Outputs:
- new_centroids: bfloat16 [256, 256, 768], P('cluster', 'dp')
- point_score: float32 [524288], P(('dp', 'cluster'))
Inputs may be any that keep to these rules, and one draw needn't show every extreme that they name: `coarse_id`: in the rows of one device no coarse cluster appears more than 24 times, and some cluster appears exactly 24 times. `owner_map`: a permutation; slot s lies on cluster index s // 16.
All inputs are finite; a program needn't handle non-finite values.
Results may differ from a plain program's by a relative error of at most 0.007.
Values may be sent and summed in bfloat16 or wider, within the bound.
No kernel may reach another device: no remote copies, remote signals or barrier semaphores. Data moves between devices by JAX's collectives and lax.ppermute only.
A program may use at most 128 MiB of HBM per device.

v0:
```python
import jax
import jax.numpy as jnp
from jax import lax
from jax.sharding import PartitionSpec as P

prior_mass = 4.0


def local(points, coarse_id, owner_map, centroids):
    slots_dev = centroids.shape[0]
    feature_width = points.shape[1]
    cluster_count = lax.axis_size("cluster")
    total_slots = owner_map.shape[0]
    point_rows = points.shape[0]
    capacity = 3 * point_rows // total_slots
    coarse = coarse_id[:, 0]
    slot_ids = jnp.arange(total_slots, dtype=jnp.int32)
    lookup = coarse[:, None] == slot_ids[None, :]
    slot_index = jnp.sum(jnp.where(lookup, owner_map[None, :], 0), axis=1)
    slot_hits = (slot_index[:, None] == slot_ids[None, :]).astype(jnp.int32)
    position_in = jnp.sum((jnp.cumsum(slot_hits, 0) - 1) * slot_hits, axis=1)
    placement = slot_index * capacity + position_in
    outbound = (
        jnp.zeros((total_slots * capacity, feature_width), jnp.bfloat16).at[placement].set(points)
    )
    filled = (
        jnp.zeros((total_slots * capacity,), jnp.bfloat16)
        .at[placement]
        .set(jnp.ones((point_rows,), jnp.bfloat16))
    )
    panels = lax.all_gather(centroids, "dp", axis=1, tiled=True)
    inbound, present = (
        lax.all_to_all(outbound, "cluster", split_axis=0, concat_axis=0, tiled=True),
        lax.all_to_all(filled, "cluster", split_axis=0, concat_axis=0, tiled=True),
    )
    arrived = inbound.reshape(cluster_count, slots_dev, capacity, feature_width)
    present_mask = present.reshape(cluster_count, slots_dev, capacity)
    sqnorm = jnp.sum(jnp.square(panels.astype(jnp.float32)), -1)
    logits = (
        jnp.einsum("sjcd,jfd->sjcf", arrived, panels, preferred_element_type=jnp.float32)
        - 0.5 * sqnorm[None, :, None, :]
    )
    row_peak = jnp.max(logits, -1, keepdims=True)
    shifted = jnp.exp(logits - row_peak)
    row_total = jnp.sum(shifted, -1, keepdims=True)
    log_total = row_peak[..., 0] + jnp.log(row_total[..., 0])
    weights_bf = (shifted / row_total).astype(jnp.bfloat16) * present_mask[..., None]
    returned = lax.all_to_all(
        log_total.reshape(-1), "cluster", split_axis=0, concat_axis=0, tiled=True
    )
    point_score = returned[placement]
    weighted = jnp.einsum("sjcf,sjcd->jfd", weights_bf, arrived, preferred_element_type=jnp.float32)
    counts = jnp.sum(weights_bf.astype(jnp.float32), axis=(0, 2))
    weighted_part, counts_part = (
        lax.psum_scatter(weighted, "dp", scatter_dimension=1, tiled=True),
        lax.psum_scatter(counts, "dp", scatter_dimension=1, tiled=True),
    )
    updated = (
        (weighted_part + prior_mass * centroids.astype(jnp.float32))
        / (counts_part[..., None] + prior_mass)
    ).astype(jnp.bfloat16)
    return (updated, point_score)


def solution(mesh):
    placed = (P(("dp", "cluster"), None), P(("dp", "cluster"), None), P(), P("cluster", "dp", None))
    return jax.shard_map(
        local,
        mesh=mesh,
        in_specs=placed,
        out_specs=(P("cluster", "dp", None), P(("dp", "cluster"))),
        check_vma=False,
    )
```

profile of v0, /device:TPU:32, one launch (start us, length us, event | category | flops | bytes accessed | tf_op | source)
XLA Modules:
  0.0 407.8 jit_solution(2727471434417005122)
XLA Ops:
  7.2 1.4 select_reduce_fusion
  8.6 0.1 copy.13
  8.7 0.3 fusion.14
  9.1 0.3 add_add_fusion
  9.4 1.2 copy.14
  10.6 0.9 fusion.13
  11.6 14.6 %scatter_custom_fusion.1 = bf16[6144]{0:T(1024)(128)(2,1)S(1)} fusion(s32[2048]{0:T(1024)S(1)} %bitcast.51, bf16[2048]{0:T(1024)(128)(2,1)S(1)} %broadcast.64, bf16[]{:T(256)} %constant.10.clone.1), kind=kCustom, calls=%fused_computation.36 | custom fusion | bytes 12290 | tf_op jit(solution)/shard_map/scatter | solution.py:29
  26.2 0.5 broadcast.74
  26.7 0.7 reduce.2
  27.4 0.7 reshape.130
  28.1 8.6 %all-to-all-start.1 = ((bf16[16,2,192]{2,1,0:T(2,128)(2,1)}), bf16[16,2,192]{2,1,0:T(2,128)(2,1)S(1)}, u32[]{:S(2)}, u32[]{:S(2)}) async-start(bf16[16,2,192]{2,1,0:T(2,128)(2,1)} %reshape.130), calls=%async_computation.1 | async-start | bytes 32768 | tf_op jit(solution)/shard_map/all_to_all | solution.py:34
  36.7 15.7 %scatter_custom_fusion = bf16[6144,768]{1,0:T(8,128)(2,1)} fusion(s32[2048]{0:T(1024)S(1)} %bitcast.52, bf16[2048,768]{1,0:T(8,128)(2,1)} %param.4, bf16[]{:T(256)} %constant.10.clone.1), kind=kCustom, calls=%fused_computation.15 | custom fusion | bytes 9437696 | tf_op jit(solution)/shard_map/scatter | solution.py:24
  52.4 0.0 all-to-all-done.1
  52.4 7.2 %all-to-all-start = ((bf16[16,384,768]{2,1,0:T(8,128)(2,1)}), bf16[16,384,768]{2,1,0:T(8,128)(2,1)}, u32[]{:S(2)}, u32[]{:S(2)}) async-start(bf16[16,384,768]{2,1,0:T(8,128)(2,1)} %bitcast.47), calls=%async_computation | async-start | bytes 18874368 | tf_op jit(solution)/shard_map/all_to_all | solution.py:33
  59.6 0.0 all-gather.2.cloned.1.call-start
  59.7 0.7 all-gather.2.cloned.1.call-update
  60.3 0.0 reduce-scatter.3.cloned.1.call-start
  60.4 0.1 reshape.131
  60.5 0.1 bitcast_reduce_fusion.1
  60.6 0.1 mul.49
  60.7 69.4 %all-gather.2.cloned.1.call-done = bf16[16,256,768]{2,1,0:T(8,128)(2,1)} async-done(((bf16[16,16,768]{2,1,0:T(8,128)(2,1)}), bf16[16,256,768]{2,1,0:T(8,128)(2,1)}) %all-gather.2.cloned.1.call-update) | async-done | bytes 6291472 | tf_op jit(solution)/shard_map/all_gather | solution.py:31
  130.1 4.1 %multiply_reduce_fusion = f32[16,256]{1,0:T(8,128)S(1)} fusion(bf16[16,256,768]{2,1,0:T(8,128)(2,1)} %all-gather.2.cloned.1.call-done), kind=kLoop, calls=%fused_computation.3 | loop fusion | flops 9433088 | bytes 6307840 | tf_op jit(solution)/shard_map/reduce_sum | solution.py:38
  134.2 130.2 %all-to-all-done = bf16[16,384,768]{2,1,0:T(8,128)(2,1)} async-done(((bf16[16,384,768]{2,1,0:T(8,128)(2,1)}), bf16[16,384,768]{2,1,0:T(8,128)(2,1)}, u32[]{:S(2)}, u32[]{:S(2)}) %all-to-all-start) | async-done | bytes 9437216 | tf_op jit(solution)/shard_map/all_to_all | solution.py:33
  264.3 10.8 %bitcast_reduce_fusion = (f32[16,16,24]{2,0,1:T(8,128)S(1)}, f32[16,16,24,256]{3,2,1,0:T(8,128)}) fusion(f32[16,256]{1,0:T(8,128)S(1)} %broadcast_multiply_fusion, bf16[16,256,768]{2,1,0:T(8,128)(2,1)} %all-gather.2.cloned.1.call-done, bf16[16,16,24,768]{3,2,1,0:T(8,128)(2,1)} %bitcast.8), kind=kOutput, calls=%fused_computation.10 | convolution fusion | flops 2419058688 | bytes 22061056 | tf_op jit(solution)/shard_map/sjcd,jfd->sjcf/dot_general | solution.py:40
  275.2 0.0 copy-start
  275.2 4.3 %fusion.6 = f32[16,16,24]{2,0,1:T(8,128)S(1)} fusion(f32[16,16,24,256]{3,2,1,0:T(8,128)} %get-tuple-element.5, f32[16,16,24]{2,0,1:T(8,128)S(1)} %get-tuple-element.4, f32[16,256]{1,0:T(8,128)S(1)} %broadcast_multiply_fusion), kind=kLoop, calls=%fused_computation.14 | loop fusion | flops 4712448 | bytes 6356992 | tf_op jit(solution)/shard_map/reduce_sum | solution.py:45
  279.5 0.3 copy-done
  279.8 3.1 convert_reduce_fusion
  283.0 10.1 %fusion.9 = f32[16,256,768]{2,1,0:T(8,128)} fusion(bf16[16,16,24,256]{3,2,0,1:T(8,128)(2,1)S(1)} %get-tuple-element.3, bf16[16,16,24,768]{3,2,1,0:T(8,128)(2,1)} %bitcast.8), kind=kOutput, calls=%fused_computation.17 | convolution fusion | flops 2415919104 | bytes 25165824 | tf_op jit(solution)/shard_map/sjcf,sjcd->jfd/dot_general | solution.py:52
  293.0 0.0 copy-start.2
  293.0 0.0 reduce-scatter.3.cloned.1.call-update
  293.1 0.0 copy-start.1
  293.1 0.6 copy-done.2
  293.7 0.6 dynamic-slice
  295.0 0.7 add.64
  295.8 6.7 %all-to-all-start.2 = ((f32[16,384,1]{1,2,0:T(1,128)}), f32[16,384,1]{1,2,0:T(1,128)S(1)}, u32[]{:S(2)}, u32[]{:S(2)}) async-start(f32[16,384,1]{1,2,0:T(1,128)} %add.64), calls=%async_computation.3 | async-start | bytes 49152 | tf_op jit(solution)/shard_map/all_to_all | solution.py:48
  302.5 75.8 %all-reduce = f32[16,256]{1,0:T(8,128)S(1)} all-reduce(f32[16,256]{1,0:T(8,128)S(1)} %get-tuple-element.2), channel_id=3, replica_groups=mesh['dp'=16,'cluster'=16] {'dp'}, use_global_device_ids=true, to_apply=%region_11.12.clone | all-reduce | flops 4096 | bytes 32768
  378.3 0.1 dynamic-slice_add_fusion
  378.4 0.0 all-to-all-done.2
  378.4 20.5 %gather_fusion = f32[2048]{0:T(1024)} fusion(f32[6144]{0:T(1024)S(1)} %bitcast.46, s32[2048]{0:T(1024)S(1)} %broadcast_clamp_fusion), kind=kCustom, calls=%fused_computation | custom fusion | bytes 24576 | tf_op jit(solution)/shard_map/gather | solution.py:51
  399.0 0.0 reduce-scatter.3.cloned.1.call-done
  399.0 0.0 copy-done.1
  399.0 2.0 divide_convert_fusion.1
  (12 shorter events, 0.2 us)
Async XLA Ops:
  28.1 24.3 %all-to-all-start.1 = ((bf16[16,2,192]{2,1,0:T(2,128)(2,1)}), bf16[16,2,192]{2,1,0:T(2,128)(2,1)S(1)}, u32[]{:S(2)}, u32[]{:S(2)}) async-start(bf16[16,2,192]{2,1,0:T(2,128)(2,1)} %reshape.130), calls=%async_computation.1 | async-start | bytes 32768 | tf_op jit(solution)/shard_map/all_to_all | solution.py:34
  52.4 212.0 %all-to-all-start = ((bf16[16,384,768]{2,1,0:T(8,128)(2,1)}), bf16[16,384,768]{2,1,0:T(8,128)(2,1)}, u32[]{:S(2)}, u32[]{:S(2)}) async-start(bf16[16,384,768]{2,1,0:T(8,128)(2,1)} %bitcast.47), calls=%async_computation | async-start | bytes 18874368 | tf_op jit(solution)/shard_map/all_to_all | solution.py:33
  59.6 70.5 %all-gather.2.cloned.1.call-start = ((), (), s32[]{:S(2)}) async-start(), calls=%async_computation.4 | async-start | bytes 6684672 | tf_op jit(solution)/shard_map/all_gather | solution.py:31
  60.3 338.6 %reduce-scatter.3.cloned.1.call-start = ((), (), s32[]{:S(2)}) async-start(), calls=%async_computation.5 | async-start | bytes 13369344 | tf_op jit(solution)/shard_map/reduce_scatter | solution.py:55
  275.2 4.6 %copy-start = (f32[16,16,24,256]{3,2,1,0:T(8,128)S(1)}, f32[16,16,24,256]{3,2,1,0:T(8,128)}, u32[]{:S(2)}) copy-start(f32[16,16,24,256]{3,2,1,0:T(8,128)} %get-tuple-element.5) | copy-start | bytes 18874372
  293.0 0.7 copy-start.2
  293.1 105.9 %copy-start.1 = (bf16[16,16,768]{2,1,0:T(8,128)(2,1)S(1)}, bf16[16,16,768]{2,1,0:T(8,128)(2,1)}, u32[]{:S(2)}) copy-start(bf16[16,16,768]{2,1,0:T(8,128)(2,1)} %param.7) | copy-start | bytes 1179652
  295.8 82.6 %all-to-all-start.2 = ((f32[16,384,1]{1,2,0:T(1,128)}), f32[16,384,1]{1,2,0:T(1,128)S(1)}, u32[]{:S(2)}, u32[]{:S(2)}) async-start(f32[16,384,1]{1,2,0:T(1,128)} %add.64), calls=%async_computation.3 | async-start | bytes 49152 | tf_op jit(solution)/shard_map/all_to_all | solution.py:48
Sparse Core Ops, SparseCore 0:
  62.8 67.1 all-gather.1
  293.2 101.0 reduce-scatter.2
where the time goes:
time: 408 us
  waiting for transfers between devices  200 us (49%)
  blocking collectives  75.8 us (19%)
  local copies, waits for them, and re-layouts  56.1 us (14%)
  starting transfers between devices  22.6 us (6%)
  matrix products  20.9 us (5%)
  other arithmetic  17.3 us (4%)
  between operations  14.9 us (4%)
    all_to_all x1, waiting for transfers between devices, local(): lax.all_to_all(outbound, 'cluster', split_axis=0, concat_axis=0, tiled=True)  130 us
    unnamed x1, blocking collectives  75.8 us
    all_gather x1, waiting for transfers between devices, local(): panels = lax.all_gather(centroids, 'dp', axis=1, tiled=True)  69.4 us
    gather x1, local copies, waits for them, and re-layouts, local(): point_score = returned[placement]  20.5 us
    scatter x1, local copies, waits for them, and re-layouts, local(): jnp.zeros((total_slots * capacity, feature_width), jnp.bfloat16)  15.7 us
    scatter x1, local copies, waits for them, and re-layouts, local(): filled = jnp.zeros((total_slots * capacity,), jnp.bfloat16).at[placement]...  14.6 us
    dot_general x1, matrix products, local(): jnp.einsum('sjcd,jfd->sjcf', arrived, panels, preferred_element_type=jnp....  10.8 us
    dot_general x1, matrix products, local(): jnp.einsum('sjcf,sjcd->jfd', weights_bf, arrived, preferred_element_type=...  10.1 us
  transfers between devices with their start and end apart: 5, of which 2 were waited for; matrix products, arithmetic and copies ran while one was open for 10% of the time, Pallas kernels for 0%

commit v1 on v0

--- a/solution.py
+++ b/solution.py
@@ -28,7 +28,9 @@
         .at[placement]
         .set(jnp.ones((point_rows,), jnp.bfloat16))
     )
-    panels = lax.all_gather(centroids, "dp", axis=1, tiled=True)
+    panels = jnp.concatenate(
+        lax.all_to_all(jnp.stack([centroids] * lax.axis_size("dp")), "dp", 0, 0), axis=1
+    )
     inbound, present = (
         lax.all_to_all(outbound, "cluster", split_axis=0, concat_axis=0, tiled=True),
         lax.all_to_all(filled, "cluster", split_axis=0, concat_axis=0, tiled=True),

time: 408 us -> 499 us (1.22)
  waiting for transfers between devices: 200 us -> 272 us
  blocking collectives: 75.8 us -> 87.7 us
  local copies, waits for them, and re-layouts: 56.1 us -> 65.1 us
    all_to_all x1, waiting for transfers between devices: 0.01 us -> 78.4 us  [local(): lax.all_to_all(jnp.stack([centroids] * lax.axis_size('dp')), 'dp', 0, 0)]
    all_gather x1 -> x0, waiting for transfers between devices: 69.4 us -> none  [local(): panels = lax.all_gather(centroids, 'dp', axis=1, tiled=True)]
    all_to_all x1, waiting for transfers between devices: 130 us -> 194 us  [local(): lax.all_to_all(outbound, 'cluster', split_axis=0, concat_axis=0, tiled=True)]
    all_to_all x0 -> x1, blocking collectives: none -> 14.6 us  [local(): lax.all_to_all(filled, 'cluster', split_axis=0, concat_axis=0, tiled=True)]
    reshape x0 -> x1, local copies, waits for them, and re-layouts: none -> 6.19 us  [local(): jnp.concatenate(lax.all_to_all(jnp.stack([centroids] * lax.axis_size('dp'...]
  transfers between devices with their start and end apart: 5 -> 4, of which waited for: 2 -> 2; matrix products, arithmetic and copies ran while one was open for 10% -> 10% of each run, Pallas kernels for 0% -> 0%
where the time goes in v1:
time: 499 us; the launch traced here: 498 us
  waiting for transfers between devices  272 us (55%)
  blocking collectives  87.7 us (18%)
  local copies, waits for them, and re-layouts  65.1 us (13%)
  matrix products  20.9 us (4%)
  starting transfers between devices  20.1 us (4%)
  other arithmetic  17.3 us (3%)
  between operations  14.9 us (3%)
    all_to_all x1, waiting for transfers between devices, local(): lax.all_to_all(outbound, 'cluster', split_axis=0, concat_axis=0, tiled=True)  194 us
    all_to_all x1, waiting for transfers between devices, local(): lax.all_to_all(jnp.stack([centroids] * lax.axis_size('dp')), 'dp', 0, 0)  78.4 us
    unnamed x1, blocking collectives  73.1 us
    gather x1, local copies, waits for them, and re-layouts, local(): point_score = returned[placement]  20.5 us
    scatter x1, local copies, waits for them, and re-layouts, local(): jnp.zeros((total_slots * capacity, feature_width), jnp.bfloat16)  15.7 us
    all_to_all x1, blocking collectives, local(): lax.all_to_all(filled, 'cluster', split_axis=0, concat_axis=0, tiled=True)  14.6 us
    scatter x1, local copies, waits for them, and re-layouts, local(): filled = jnp.zeros((total_slots * capacity,), jnp.bfloat16).at[placement]...  14.6 us
    dot_general x1, matrix products, local(): jnp.einsum('sjcd,jfd->sjcf', arrived, panels, preferred_element_type=jnp....  10.8 us
  transfers between devices with their start and end apart: 4, of which 2 were waited for; matrix products, arithmetic and copies ran while one was open for 10% of the time, Pallas kernels for 0%

profile of v1, /device:TPU:32, one launch (start us, length us, event | category | flops | bytes accessed | tf_op | source)
XLA Modules:
  0.0 498.1 jit_solution(5344813668684489611)
XLA Ops:
  7.2 1.4 select_reduce_fusion
  8.6 0.1 copy.31
  8.7 0.0 copy-start.1
  8.7 0.3 fusion.13
  9.1 0.3 add_add_fusion
  9.4 1.2 copy.32
  10.6 0.9 fusion.12
  11.6 14.6 %scatter_custom_fusion.1 = bf16[6144]{0:T(1024)(128)(2,1)S(1)} fusion(s32[2048]{0:T(1024)S(1)} %bitcast.53, bf16[2048]{0:T(1024)(128)(2,1)S(1)} %broadcast.68, bf16[]{:T(256)} %constant.10.clone.1), kind=kCustom, calls=%fused_computation.35 | custom fusion | bytes 12290 | tf_op jit(solution)/shard_map/scatter | solution.py:29
  26.2 0.5 broadcast.78
  26.7 0.7 reduce.3
  27.4 0.1 reshape.146
  27.5 14.6 %all_to_all.33 = bf16[16,2,192]{2,1,0:T(2,128)(2,1)S(1)} all-to-all(bf16[16,2,192]{2,1,0:T(2,128)(2,1)S(1)} %reshape.146), channel_id=1, replica_groups=mesh['dp'=16,'cluster'=16] {'cluster'}, dimensions={0} | all-to-all | bytes 24576 | tf_op jit(solution)/shard_map/all_to_all | solution.py:36
  42.1 0.0 copy-done.1
  42.1 3.3 stack.2
  45.4 7.1 %all-to-all-start.1 = ((bf16[16,16,16,768]{3,2,1,0:T(8,128)(2,1)}), bf16[16,16,16,768]{3,2,1,0:T(8,128)(2,1)}, u32[]{:S(2)}, u32[]{:S(2)}) async-start(bf16[16,16,16,768]{3,2,1,0:T(8,128)(2,1)} %stack.2), calls=%async_computation.1 | async-start | bytes 12582912 | tf_op jit(solution)/shard_map/all_to_all | solution.py:32
  52.5 15.7 %scatter_custom_fusion = bf16[6144,768]{1,0:T(8,128)(2,1)} fusion(s32[2048]{0:T(1024)S(1)} %bitcast.54, bf16[2048,768]{1,0:T(8,128)(2,1)} %param.4, bf16[]{:T(256)} %constant.10.clone.1), kind=kCustom, calls=%fused_computation.14 | custom fusion | bytes 9437696 | tf_op jit(solution)/shard_map/scatter | solution.py:24
  68.2 78.4 %all-to-all-done.1 = bf16[16,16,16,768]{3,2,1,0:T(8,128)(2,1)} async-done(((bf16[16,16,16,768]{3,2,1,0:T(8,128)(2,1)}), bf16[16,16,16,768]{3,2,1,0:T(8,128)(2,1)}, u32[]{:S(2)}, u32[]{:S(2)}) %all-to-all-start.1) | async-done | bytes 6291488 | tf_op jit(solution)/shard_map/all_to_all | solution.py:32
  146.6 6.0 %all-to-all-start = ((bf16[16,384,768]{2,1,0:T(8,128)(2,1)}), bf16[16,384,768]{2,1,0:T(8,128)(2,1)}, u32[]{:S(2)}, u32[]{:S(2)}) async-start(bf16[16,384,768]{2,1,0:T(8,128)(2,1)} %bitcast.48), calls=%async_computation | async-start | bytes 18874368 | tf_op jit(solution)/shard_map/all_to_all | solution.py:35
  152.6 0.3 reduce-scatter.3.cloned.1.call-start
  152.8 0.1 reshape.147
  152.9 0.1 bitcast_reduce_fusion.1
  153.0 0.1 mul.53
  153.2 4.1 multiply_reduce_fusion
  157.3 0.1 mul.52
  157.4 6.2 %copy.33 = bf16[16,16,16,768]{3,2,1,0:T(8,128)(2,1)} copy(bf16[16,16,16,768]{3,2,0,1:T(8,128)(2,1)} %bitcast.9) | data formatting | bytes 12582912 | tf_op jit(solution)/shard_map/reshape | solution.py:31
  163.6 193.7 %all-to-all-done = bf16[16,384,768]{2,1,0:T(8,128)(2,1)} async-done(((bf16[16,384,768]{2,1,0:T(8,128)(2,1)}), bf16[16,384,768]{2,1,0:T(8,128)(2,1)}, u32[]{:S(2)}, u32[]{:S(2)}) %all-to-all-start) | async-done | bytes 9437216 | tf_op jit(solution)/shard_map/all_to_all | solution.py:35
  357.3 10.8 %bitcast_reduce_fusion = (f32[16,16,24]{2,0,1:T(8,128)S(1)}, f32[16,16,24,256]{3,2,1,0:T(8,128)}) fusion(f32[16,256]{1,0:T(8,128)S(1)} %mul.52, bf16[16,256,768,1]{2,1,3,0:T(8,128)(2,1)} %bitcast.49, bf16[16,16,24,768]{3,2,1,0:T(8,128)(2,1)} %bitcast.8), kind=kOutput, calls=%fused_computation.9 | convolution fusion | flops 2419058688 | bytes 22061056 | tf_op jit(solution)/shard_map/sjcd,jfd->sjcf/dot_general | solution.py:42
  368.1 0.0 copy-start
  368.1 4.3 fusion.5
  372.4 0.3 copy-done
  372.8 3.1 convert_reduce_fusion
  375.9 10.1 %fusion.8 = f32[16,256,768]{2,1,0:T(8,128)} fusion(bf16[16,16,24,256]{3,2,0,1:T(8,128)(2,1)S(1)} %get-tuple-element.3, bf16[16,16,24,768]{3,2,1,0:T(8,128)(2,1)} %bitcast.8), kind=kOutput, calls=%fused_computation.16 | convolution fusion | flops 2415919104 | bytes 25165824 | tf_op jit(solution)/shard_map/sjcf,sjcd->jfd/dot_general | solution.py:54
  386.0 0.0 copy-start.2
  386.0 0.0 reduce-scatter.3.cloned.1.call-update
  386.0 0.6 copy-done.2
  386.7 0.6 dynamic-slice
  388.0 0.7 add.64
  388.8 6.8 %all-to-all-start.3 = ((f32[16,384,1]{1,2,0:T(1,128)}), f32[16,384,1]{1,2,0:T(1,128)S(1)}, u32[]{:S(2)}, u32[]{:S(2)}) async-start(f32[16,384,1]{1,2,0:T(1,128)} %add.64), calls=%async_computation.4 | async-start | bytes 49152 | tf_op jit(solution)/shard_map/all_to_all | solution.py:50
  395.5 73.1 %all-reduce = f32[16,256]{1,0:T(8,128)S(1)} all-reduce(f32[16,256]{1,0:T(8,128)S(1)} %get-tuple-element.2), channel_id=3, replica_groups=mesh['dp'=16,'cluster'=16] {'dp'}, use_global_device_ids=true, to_apply=%region_11.12.clone | all-reduce | flops 4096 | bytes 32768
  468.6 0.1 dynamic-slice_add_fusion
  468.7 0.0 all-to-all-done.3
  468.7 20.5 %gather_fusion = f32[2048]{0:T(1024)} fusion(f32[6144]{0:T(1024)S(1)} %bitcast.47, s32[2048]{0:T(1024)S(1)} %broadcast_clamp_fusion), kind=kCustom, calls=%fused_computation | custom fusion | bytes 24576 | tf_op jit(solution)/shard_map/gather | solution.py:53
  489.2 0.0 reduce-scatter.3.cloned.1.call-done
  489.2 2.0 divide_convert_fusion.1
  (13 shorter events, 0.2 us)
Async XLA Ops:
  8.7 33.4 %copy-start.1 = (bf16[16,16,768]{2,1,0:T(8,128)(2,1)S(1)}, bf16[16,16,768]{2,1,0:T(8,128)(2,1)}, u32[]{:S(2)}) copy-start(bf16[16,16,768]{2,1,0:T(8,128)(2,1)} %param.7) | copy-start | bytes 1179652
  45.4 101.2 %all-to-all-start.1 = ((bf16[16,16,16,768]{3,2,1,0:T(8,128)(2,1)}), bf16[16,16,16,768]{3,2,1,0:T(8,128)(2,1)}, u32[]{:S(2)}, u32[]{:S(2)}) async-start(bf16[16,16,16,768]{3,2,1,0:T(8,128)(2,1)} %stack.2), calls=%async_computation.1 | async-start | bytes 12582912 | tf_op jit(solution)/shard_map/all_to_all | solution.py:32
  146.6 210.7 %all-to-all-start = ((bf16[16,384,768]{2,1,0:T(8,128)(2,1)}), bf16[16,384,768]{2,1,0:T(8,128)(2,1)}, u32[]{:S(2)}, u32[]{:S(2)}) async-start(bf16[16,384,768]{2,1,0:T(8,128)(2,1)} %bitcast.48), calls=%async_computation | async-start | bytes 18874368 | tf_op jit(solution)/shard_map/all_to_all | solution.py:35
  152.6 336.7 %reduce-scatter.3.cloned.1.call-start = ((), (), s32[]{:S(2)}) async-start(), calls=%async_computation.5 | async-start | bytes 13369344 | tf_op jit(solution)/shard_map/reduce_scatter | solution.py:57
  368.1 4.6 copy-start
  386.0 0.7 copy-start.2
  388.8 79.9 %all-to-all-start.3 = ((f32[16,384,1]{1,2,0:T(1,128)}), f32[16,384,1]{1,2,0:T(1,128)S(1)}, u32[]{:S(2)}, u32[]{:S(2)}) async-start(f32[16,384,1]{1,2,0:T(1,128)} %add.64), calls=%async_computation.4 | async-start | bytes 49152 | tf_op jit(solution)/shard_map/all_to_all | solution.py:50
Sparse Core Ops, SparseCore 0:
  386.1 99.3 reduce-scatter.2
